TPU v7x, 32 devices: a whole 2x2x4 slice. The times are simulated.
32 devices in a mesh: seq: 8 (over y, x, core), exp: 4 (over z).
Axes of the slice: x: 2, y: 2, z: 4, core: 2. Of those that a mesh axis runs over, the one named last changes fastest.
Arguments:
- layer_input: bfloat16 [4, 4096, 768], P('exp', 'seq'), may hold values from -6 to 6
- token_ids: int32 [4, 4096], P('exp', 'seq'), may hold values from 0 to 8007, as said below
- segment_ids: int32 [4, 4096], P('exp'), may hold values from 0 to 7, never falling along the last dimension, each value on 1 to 1024 neighbouring positions
- hash_table: int32 [8008], replicated, may hold values from 0 to 3, as said below
- first_gain: float32 [768], replicated, may hold values from 0.25 to 1.75
- first_bias: float32 [768], replicated, may hold values from -1.5 to 1.5
- second_gain: float32 [768], replicated, may hold values from 0.25 to 1.75
- second_bias: float32 [768], replicated, may hold values from -1.5 to 1.5
- w_qkv: bfloat16 [768, 2304], replicated, may hold values from -0.21875 to 0.21875
- w_out: bfloat16 [768, 768], replicated, may hold values from -3 to 3
- w_up: bfloat16 [4, 768, 3072], P('exp'), may hold values from -0.21875 to 0.21875
- w_down: bfloat16 [4, 3072, 768], P('exp'), may hold values from -0.109375 to 0.109375
- cotangent: bfloat16 [4, 4096, 768], P('exp', 'seq'), may hold values from -6 to 6
Outputs:
- layer_output: bfloat16 [4, 4096, 768], P('exp', 'seq')
- grad_input: float32 [4, 4096, 768], P('exp', 'seq')
- grad_w_qkv: float32 [768, 2304], replicated
- grad_w_out: float32 [768, 768], replicated
- grad_first_gain: float32 [768], replicated
- grad_first_bias: float32 [768], replicated
- grad_second_gain: float32 [768], replicated
- grad_second_bias: float32 [768], replicated
- grad_w_up: float32 [4, 768, 3072], P('exp')
- grad_w_down: float32 [4, 3072, 768], P('exp')
Inputs may be any that keep to these rules, and one draw needn't show every extreme that they name: `token_ids`: token ids range over the vocabulary. Among the 512 positions that one device holds, hash_table sends exactly 256 to one expert, the same expert on all devices that hold the same positions of their sequences, and the other experts' counts differ from one another by at most one. `hash_table`: every expert is named by 2002 token ids. `segment_ids`: numbers never fall along a sequence; each document holds 1 to 1024 neighbouring positions, and one in every sequence holds exactly 1024.
All inputs are finite; a program needn't handle non-finite values.
Results may differ from a plain program's by a relative error of at most 0.017.
Values may be sent and summed in bfloat16 or wider, within the bound.
No kernel may reach another device: no remote copies, remote signals or barrier semaphores. Data moves between devices by JAX's collectives and lax.ppermute only.
A program may use at most 192 MiB of HBM per device.

v0:
```python
import math
import jax
import jax.numpy as jnp
from jax import lax
from jax.sharding import PartitionSpec as P

HEADS = 12
HEAD_DIM = 64
DOC_MOST = 1024
NEG_BIG = -1e30
EPSILON = 1e-05


def passed_along(block, axis, distance):
    devices = range(lax.axis_size(axis))
    route = [(i - distance, i) for i in devices if i - distance in devices]
    return lax.ppermute(block, axis, route)


def smooth_gate(values):
    return jax.nn.gelu(values, approximate=True)


def norm_rows(values):
    center = values - jnp.mean(values, axis=-1, keepdims=True)
    scale = lax.rsqrt(jnp.mean(center * center, axis=-1, keepdims=True) + EPSILON)
    return (center * scale, scale)


def norm_back(grad_normed, normed, scale):
    inner = jnp.mean(grad_normed * normed, axis=-1, keepdims=True)
    return scale * (grad_normed - jnp.mean(grad_normed, axis=-1, keepdims=True) - normed * inner)


def over_blocks(step, state, pieces, first):
    length = pieces[0].shape[0]
    stride = math.gcd(length, 512)

    def advance(index, current):
        begin = index * stride
        parts = tuple((piece for piece in pieces))
        return step(current, parts, first + begin)

    return lax.fori_loop(0, length // stride, advance, state)


def allowed_pairs(query_pos, query_seg, key_pos, key_seg, limit):
    inside = (key_pos[None, :] >= 0) & (query_pos[:, None] < limit)
    return (
        inside & (key_pos[None, :] <= query_pos[:, None]) & (key_seg[None, :] == query_seg[:, None])
    )


def head_split(rows):
    return rows.reshape(rows.shape[0], HEADS, HEAD_DIM)


def forward_step(queries, query_pos, query_seg, segment_row, limit):
    width = HEADS * HEAD_DIM
    scale = HEAD_DIM ** (-0.5)

    def step(state, parts, first):
        run_max, run_total, weighted = state
        count = parts[0].shape[0]
        key_rows = head_split(parts[0][:, :width])
        value_rows = head_split(parts[0][:, width:])
        key_pos = first + jnp.arange(count, dtype=jnp.int32)
        key_seg = lax.dynamic_slice_in_dim(segment_row, first, count, 0)
        allowed = allowed_pairs(query_pos, query_seg, key_pos, key_seg, limit)[None]
        scores = (
            jnp.einsum("qhd,khd->hqk", queries, key_rows, preferred_element_type=jnp.float32)
            * scale
        )
        new_max = jnp.maximum(run_max, jnp.max(jnp.where(allowed, scores, NEG_BIG), axis=-1))
        shares = jnp.where(allowed, jnp.exp(scores - new_max[..., None]), 0.0)
        factor = jnp.exp(run_max - new_max)
        run_total = run_total * factor + jnp.sum(shares, axis=-1)
        update = jnp.einsum(
            "hqk,khd->qhd",
            shares.astype(jnp.bfloat16),
            value_rows,
            preferred_element_type=jnp.float32,
        )
        weighted = weighted * factor.T[:, :, None] + update
        return (new_max, run_total, weighted)

    return step


def backward_core(queries, grad_heads, log_total, delta, key_rows, value_rows, allowed):
    scale = HEAD_DIM ** (-0.5)
    scores = (
        jnp.einsum("qhd,khd->hqk", queries, key_rows, preferred_element_type=jnp.float32) * scale
    )
    soft = jnp.where(allowed[None], jnp.exp(scores - log_total[..., None]), 0.0)
    grad_soft = jnp.einsum(
        "qhd,khd->hqk", grad_heads, value_rows, preferred_element_type=jnp.float32
    )
    grad_scores = (soft * (grad_soft - delta[..., None])).astype(jnp.bfloat16)
    return (soft.astype(jnp.bfloat16), grad_scores)


def query_step(queries, grad_heads, log_total, delta, query_pos, query_seg, segment_row, limit):
    width = HEADS * HEAD_DIM
    scale = HEAD_DIM ** (-0.5)

    def step(state, parts, first):
        count = parts[0].shape[0]
        key_rows = head_split(parts[0][:, :width])
        value_rows = head_split(parts[0][:, width:])
        key_pos = first + jnp.arange(count, dtype=jnp.int32)
        key_seg = lax.dynamic_slice_in_dim(segment_row, first, count, 0)
        allowed = allowed_pairs(query_pos, query_seg, key_pos, key_seg, limit)
        soft_low, grad_scores = backward_core(
            queries, grad_heads, log_total, delta, key_rows, value_rows, allowed
        )
        grad_query = (
            jnp.einsum("hqk,khd->qhd", grad_scores, key_rows, preferred_element_type=jnp.float32)
            * scale
        )
        grad_q, grad_block = state
        grad_keys = (
            jnp.einsum("hqk,qhd->khd", grad_scores, queries, preferred_element_type=jnp.float32)
            * scale
        )
        grad_values = jnp.einsum(
            "hqk,qhd->khd", soft_low, grad_heads, preferred_element_type=jnp.float32
        )
        joined = jnp.concatenate(
            [grad_keys.reshape(count, width), grad_values.reshape(count, width)], axis=1
        )
        current = grad_block
        grad_block = current + joined
        return (grad_q + grad_query, grad_block)

    return step


def on_device(
    layer_input,
    token_ids,
    segment_ids,
    hash_table,
    first_gain,
    first_bias,
    second_gain,
    second_bias,
    w_qkv,
    w_out,
    w_up,
    w_down,
    cotangent,
):
    local_len = layer_input.shape[1]
    width = layer_input.shape[2]
    sources = lax.axis_size("exp")
    local_exp = w_up.shape[0]
    experts_total = local_exp * sources
    capacity = 2 * local_len // experts_total
    total_len = local_len * lax.axis_size("seq")
    reach_blocks = (DOC_MOST + local_len - 2) // local_len
    offset = lax.axis_index("seq") * local_len
    segment_row = segment_ids[0]
    query_pos = offset + jnp.arange(local_len, dtype=jnp.int32)
    query_seg = lax.dynamic_slice_in_dim(segment_row, offset, local_len, 0)
    inputs = layer_input[0].astype(jnp.float32)
    normed_one, scale_one = norm_rows(inputs)
    attn_in = (normed_one * first_gain + first_bias).astype(jnp.bfloat16)
    projected = jnp.dot(attn_in, w_qkv, preferred_element_type=jnp.float32).astype(jnp.bfloat16)
    queries = head_split(projected[:, :width])
    key_value = projected[:, width:]
    kv_blocks = [key_value]
    moving = key_value
    for hop_index in range(reach_blocks):
        moving = passed_along(moving, "seq", 1)
        kv_blocks.append(moving)
    state = (
        jnp.full((HEADS, local_len), NEG_BIG, jnp.float32),
        jnp.zeros((HEADS, local_len), jnp.float32),
        jnp.zeros((local_len, HEADS, HEAD_DIM), jnp.float32),
    )
    attend = forward_step(queries, query_pos, query_seg, segment_row, total_len)
    for block_index in range(reach_blocks + 1):
        state = over_blocks(
            attend, state, (kv_blocks[block_index],), offset - block_index * local_len
        )
    run_max, run_total, weighted = state
    attn_exact = (weighted / run_total.T[:, :, None]).reshape(local_len, width)
    log_total = run_max + jnp.log(run_total)
    attn_rows = attn_exact.astype(jnp.bfloat16)
    resid = inputs + jnp.dot(attn_rows, w_out, preferred_element_type=jnp.float32)
    normed_two, scale_two = norm_rows(resid)
    ffn_in = (normed_two * second_gain + second_bias).astype(jnp.bfloat16)
    choice_ids = hash_table[token_ids[0]]
    order = jnp.argsort(choice_ids, stable=True)
    places = jnp.argsort(order, stable=True)
    expert_grid = jnp.arange(experts_total, dtype=jnp.int32)
    matches = choice_ids[:, None] == expert_grid[None, :]
    counts = jnp.sum(matches.astype(jnp.int32), axis=0)
    starts = jnp.cumsum(counts) - counts
    slot_grid = jnp.arange(capacity, dtype=jnp.int32)
    gather_index = order[jnp.minimum(starts[:, None] + slot_grid[None, :], local_len - 1)]
    filled = (slot_grid[None, :] < counts[:, None])[:, :, None]
    own_start = jnp.sum(jnp.where(matches, starts[None, :], 0), axis=1)
    token_slot = choice_ids * capacity + places - own_start
    send = jnp.where(filled, ffn_in[gather_index], jnp.zeros((), jnp.bfloat16))
    received = lax.all_to_all(send, "exp", split_axis=0, concat_axis=0, tiled=True)
    grouped = received.reshape(sources, local_exp, capacity, width)
    pre_act = jnp.einsum("secd,edf->secf", grouped, w_up, preferred_element_type=jnp.float32)
    activated, gate_pullback = jax.vjp(smooth_gate, pre_act)
    hidden = activated.astype(jnp.bfloat16)
    expert_out = jnp.einsum(
        "secf,efd->secd", hidden, w_down, preferred_element_type=jnp.float32
    ).astype(jnp.bfloat16)
    returned = lax.all_to_all(
        expert_out.reshape(experts_total, capacity, width),
        "exp",
        split_axis=0,
        concat_axis=0,
        tiled=True,
    )
    ffn_rows = returned.reshape(experts_total * capacity, width)[token_slot].astype(jnp.float32)
    layer_output = (resid + ffn_rows).astype(jnp.bfloat16)
    grad_final = cotangent[0].astype(jnp.float32)
    grad_branch = grad_final.astype(jnp.bfloat16)
    grad_send = jnp.where(filled, grad_branch[gather_index], jnp.zeros((), jnp.bfloat16))
    grad_received = lax.all_to_all(
        grad_send, "exp", split_axis=0, concat_axis=0, tiled=True
    ).reshape(sources, local_exp, capacity, width)
    grad_w_down = jnp.einsum(
        "secf,secd->efd", hidden, grad_received, preferred_element_type=jnp.float32
    )
    grad_hidden = jnp.einsum(
        "secd,efd->secf", grad_received, w_down, preferred_element_type=jnp.float32
    )
    grad_pre = gate_pullback(grad_hidden)[0].astype(jnp.bfloat16)
    grad_w_up = jnp.einsum("secd,secf->edf", grouped, grad_pre, preferred_element_type=jnp.float32)
    grad_slots = jnp.einsum(
        "secf,edf->secd", grad_pre, w_up, preferred_element_type=jnp.float32
    ).astype(jnp.bfloat16)
    grad_back = lax.all_to_all(
        grad_slots.reshape(experts_total, capacity, width),
        "exp",
        split_axis=0,
        concat_axis=0,
        tiled=True,
    )
    grad_ffn_in = grad_back.reshape(experts_total * capacity, width)[token_slot].astype(jnp.float32)
    grad_second_gain = jnp.sum(grad_ffn_in * normed_two, axis=0)
    grad_second_bias = jnp.sum(grad_ffn_in, axis=0)
    grad_resid = grad_final + norm_back(grad_ffn_in * second_gain, normed_two, scale_two)
    grad_attn = grad_resid.astype(jnp.bfloat16)
    grad_w_out = jnp.einsum("cd,ce->de", attn_rows, grad_attn, preferred_element_type=jnp.float32)
    grad_out_rows = jnp.einsum(
        "ce,de->cd", grad_attn, w_out, preferred_element_type=jnp.float32
    ).astype(jnp.bfloat16)
    grad_heads = head_split(grad_out_rows)
    delta = jnp.sum(grad_heads.astype(jnp.float32) * head_split(attn_exact), axis=-1).T
    back_blocks = [key_value]
    moving = key_value
    for hop_index in range(reach_blocks):
        moving = passed_along(moving, "seq", 1)
        back_blocks.append(moving)
    grad_query = jnp.zeros((local_len, HEADS, HEAD_DIM), jnp.float32)
    block_grads = []
    for block_index in range(reach_blocks + 1):
        base = offset - block_index * local_len
        back_step = query_step(
            queries, grad_heads, log_total, delta, query_pos, query_seg, segment_row, total_len
        )
        grad_query, grad_block = over_blocks(
            back_step,
            (grad_query, jnp.zeros((local_len, 2 * width), jnp.float32)),
            (back_blocks[block_index],),
            base,
        )
        block_grads.append(grad_block)
    carried = block_grads[reach_blocks]
    for block_index in range(reach_blocks, 0, -1):
        carried = (
            passed_along(carried.astype(jnp.bfloat16), "seq", -1).astype(carried.dtype)
            + block_grads[block_index - 1]
        )
    grad_proj = jnp.concatenate([grad_query.reshape(local_len, width), carried], axis=1).astype(
        jnp.bfloat16
    )
    grad_w_qkv = jnp.einsum("cd,ce->de", attn_in, grad_proj, preferred_element_type=jnp.float32)
    grad_attn_in = jnp.einsum("ce,de->cd", grad_proj, w_qkv, preferred_element_type=jnp.float32)
    grad_first_gain = jnp.sum(grad_attn_in * normed_one, axis=0)
    grad_first_bias = jnp.sum(grad_attn_in, axis=0)
    grad_input = grad_resid + norm_back(grad_attn_in * first_gain, normed_one, scale_one)
    dense = lax.psum(
        (
            grad_w_qkv,
            grad_w_out,
            grad_first_gain,
            grad_first_bias,
            grad_second_gain,
            grad_second_bias,
        ),
        ("seq", "exp"),
    )
    expert_sums = (
        lax.psum(grad_w_up.astype(jnp.bfloat16), "seq").astype(jnp.float32),
        lax.psum(grad_w_down.astype(jnp.bfloat16), "seq").astype(jnp.float32),
    )
    return (
        layer_output[None],
        grad_input[None],
        dense[0],
        dense[1],
        dense[2],
        dense[3],
        dense[4],
        dense[5],
        expert_sums[0],
        expert_sums[1],
    )


def solution(mesh):
    in_specs = (
        P("exp", "seq", None),
        P("exp", "seq"),
        P("exp", None),
        P(),
        P(),
        P(),
        P(),
        P(),
        P(),
        P(),
        P("exp", None, None),
        P("exp", None, None),
        P("exp", "seq", None),
    )
    out_specs = (
        P("exp", "seq", None),
        P("exp", "seq", None),
        P(),
        P(),
        P(),
        P(),
        P(),
        P(),
        P("exp", None, None),
        P("exp", None, None),
    )
    return jax.shard_map(
        on_device, mesh=mesh, in_specs=in_specs, out_specs=out_specs, check_vma=False
    )
```

profile of v0, /device:TPU:0, one launch (start us, length us, event | category | flops | bytes accessed | tf_op | source)
XLA Modules:
  0.0 691.7 jit_solution(2766946564341442537)
XLA Ops:
  10.2 3.3 convolution_convert_fusion
  16.2 3.6 collective-permute-start
  19.8 3.4 gather_fusion
  23.9 3.8 sort.31
  27.7 11.3 %gather_fusion.1 = s32[1024]{0:T(1024)} fusion(s32[512]{0:T(512)S(1)} %get-tuple-element.163, s32[1024]{0:T(1024)S(1)} %broadcast_clamp_fusion.1), kind=kCustom, calls=%fused_computation.1 | custom fusion | bytes 12288 | tf_op jit(solution)/shard_map/gather | solution.py:202
  40.5 3.1 fusion.155
  45.9 4.5 collective-permute-start.1
  56.3 2.3 copy.84
  58.6 7.0 %gather_fusion.4 = bf16[1024,768]{1,0:T(8,128)(2,1)} fusion(bf16[512,768]{1,0:T(8,128)(2,1)} %bitcast.289, s32[1024]{0:T(1024)S(1)} %broadcast_clamp_fusion), kind=kCustom, calls=%fused_computation.4 | custom fusion | bytes 3149824 | tf_op jit(solution)/shard_map/gather | solution.py:226
  65.6 8.6 %select_reduce_fusion.2 = (f32[12,512]{1,0:T(8,128)}, f32[12,512,512]{1,2,0:T(8,128)}) fusion(pred[512,512]{0,1:T(8,128)(4,1)} %get-tuple-element.239, bf16[512,12,64]{0,2,1:T(8,128)(2,1)} %bitcast.294, bf16[512,12,64]{0,2,1:T(8,128)(2,1)} %bitcast.302), kind=kOutput, calls=%fused_computation.33 | convolution fusion | flops 412084224 | bytes 14442496 | tf_op jit(solution)/shard_map/while/body/eval_jaxpr/qhd,khd->hqk/dot_general | solution.py:71
  74.2 2.6 fusion.157
  79.1 2.3 copy.89
  81.5 8.6 %select_reduce_fusion.1 = (f32[12,512]{1,0:T(8,128)}, f32[12,512,512]{1,2,0:T(8,128)}) fusion(pred[512,512]{0,1:T(8,128)(4,1)} %get-tuple-element.241, bf16[512,12,64]{0,2,1:T(8,128)(2,1)} %bitcast.295, bf16[512,12,64]{0,2,1:T(8,128)(2,1)} %bitcast.300), kind=kOutput, calls=%fused_computation.31 | convolution fusion | flops 412084224 | bytes 14442496 | tf_op jit(solution)/shard_map/while/body/eval_jaxpr/qhd,khd->hqk/dot_general | solution.py:71
  90.1 2.6 fusion.156
  97.3 8.1 %select_reduce_fusion = (f32[12,512]{1,0:T(8,128)S(1)}, f32[12,512,512]{1,2,0:T(8,128)}) fusion(pred[512,512]{0,1:T(8,128)(4,1)} %get-tuple-element.240, bf16[512,12,64]{0,2,1:T(8,128)(2,1)} %bitcast.296, bf16[512,12,64]{0,2,1:T(8,128)(2,1)} %bitcast.304), kind=kOutput, calls=%fused_computation.29 | convolution fusion | flops 412084224 | bytes 14442496 | tf_op jit(solution)/shard_map/while/body/eval_jaxpr/qhd,khd->hqk/dot_general | solution.py:71
  106.1 7.3 %fusion.13 = f32[12,512]{1,0:T(8,128)S(1)} fusion(f32[12,512,512]{1,2,0:T(8,128)} %get-tuple-element.247, f32[12,512]{1,0:T(8,128)S(1)} %get-tuple-element.210, pred[512,512]{0,1:T(8,128)(4,1)S(1)} %copy-done.19), kind=kLoop, calls=%fused_computation.36 | loop fusion | flops 12576768 | bytes 12894208 | tf_op jit(solution)/shard_map/while/body/eval_jaxpr/reduce_sum | solution.py:77
  113.4 20.8 %fusion.36 = f32[12,64,512]{2,1,0:T(8,128)} fusion(bf16[512,12,64]{0,2,1:T(8,128)(2,1)} %bitcast.324, f32[12,512,512]{1,2,0:T(8,128)} %get-tuple-element.247, f32[12,512]{1,0:T(8,128)S(1)} %get-tuple-element.210, pred[512,512]{0,1:T(8,128)(4,1)} %get-tuple-element.241), kind=kOutput, calls=%fused_computation.57 | convolution fusion | flops 415236096 | bytes 15228928 | tf_op jit(solution)/shard_map/while/body/eval_jaxpr/hqk,khd->qhd/dot_general | solution.py:78
  134.2 3.5 fusion.11
  137.8 4.7 fusion.38
  142.5 7.3 %fusion.15 = f32[12,512]{1,0:T(8,128)S(1)} fusion(f32[12,512,512]{1,2,0:T(8,128)} %get-tuple-element.245, f32[12,512]{1,0:T(8,128)} %get-tuple-element.196, pred[512,512]{0,1:T(8,128)(4,1)} %get-tuple-element.240), kind=kLoop, calls=%fused_computation.38 | loop fusion | flops 12576768 | bytes 12894208 | tf_op jit(solution)/shard_map/while/body/eval_jaxpr/reduce_sum | solution.py:77
  150.0 8.8 %fusion.158 = (bf16[512,12,64]{0,2,1:T(8,128)(2,1)S(1)}, f32[512,12,64]{0,2,1:T(8,128)}) fusion(f32[512,12]{0,1:T(8,128)S(1)} %get-tuple-element.194, bf16[512,12,64]{0,2,1:T(8,128)(2,1)S(1)} %bitcast.326, f32[12,512,512]{1,2,0:T(8,128)} %get-tuple-element.245, f32[12,512]{1,0:T(8,128)S(1)} %copy-done.37, pred[512,512]{0,1:T(8,128)(4,1)S(1)} %copy-done.21, ...), kind=kOutput, calls=%fused_computation.216 | convolution fusion | flops 417988608 | bytes 19259392 | tf_op jit(solution)/shard_map/while/body/eval_jaxpr/hqk,khd->qhd/dot_general | solution.py:78
  162.6 7.0 %gather_fusion.2 = bf16[1024,768]{1,0:T(8,128)(2,1)} fusion(bf16[512,768]{1,0:T(8,128)(2,1)} %add_convert_fusion.1, s32[1024]{0:T(1024)} %copy-done.44), kind=kCustom, calls=%fused_computation.2 | custom fusion | bytes 3149824 | tf_op jit(solution)/shard_map/gather | solution.py:206
  169.7 3.8 broadcast_select_fusion
  173.5 4.9 all-to-all-start
  179.0 4.4 sort.32
  186.3 28.2 %all-to-all-done = bf16[4,256,768]{2,1,0:T(8,128)(2,1)} async-done(((bf16[4,256,768]{2,1,0:T(8,128)(2,1)}), bf16[4,256,768]{2,1,0:T(8,128)(2,1)}, u32[]{:S(2)}, u32[]{:S(2)}) %all-to-all-start) | async-done | bytes 1572896 | tf_op jit(solution)/shard_map/all_to_all | solution.py:207
  214.5 4.4 all-to-all-start.2
  218.9 7.4 %fusion.54 = f32[4,256,3072]{2,1,0:T(8,128)S(1)} fusion(bf16[4,256,768]{2,1,0:T(8,128)(2,1)} %all-to-all-done, bf16[1,768,3072]{2,1,0:T(8,128)(2,1)} %param.23), kind=kOutput, calls=%fused_computation.69 | convolution fusion | flops 4831838208 | bytes 18874368 | tf_op jit(solution)/shard_map/secd,edf->secf/dot_general | solution.py:209
  226.3 4.5 copy-done.64
  230.7 10.8 %fusion.77 = bf16[4,256,768]{2,1,0:T(8,128)(2,1)} fusion(bf16[1,3072,768]{2,1,0:T(8,128)(2,1)} %param.24, f32[4,256,3072]{2,1,0:T(8,128)S(1)} %fusion.54), kind=kOutput, calls=%fused_computation.95 | convolution fusion | flops 4860936192 | bytes 18874368 | tf_op jit(solution)/shard_map/secf,efd->secd/dot_general | solution.py:212
  241.5 13.9 %all-to-all-done.2 = bf16[4,256,768]{2,1,0:T(8,128)(2,1)} async-done(((bf16[4,256,768]{2,1,0:T(8,128)(2,1)}), bf16[4,256,768]{2,1,0:T(8,128)(2,1)}, u32[]{:S(2)}, u32[]{:S(2)}) %all-to-all-start.2) | async-done | bytes 1572896 | tf_op jit(solution)/shard_map/all_to_all | solution.py:227
  255.4 4.8 all-to-all-start.1
  260.2 15.3 %fusion.6 = bf16[4,1,256,3072]{3,2,0,1:T(8,128)(2,1)S(1)} fusion(f32[4,256,3072]{2,1,0:T(8,128)} %copy-done.64, bf16[4,256,768]{2,1,0:T(8,128)(2,1)} %all-to-all-done.2, bf16[1,3072,768]{2,1,0:T(8,128)(2,1)} %param.24), kind=kOutput, calls=%fused_computation.14 | convolution fusion | flops 4894752768 | bytes 25165824 | tf_op jit(solution)/shard_map/secd,efd->secf/dot_general | solution.py:233
  275.5 8.5 %fusion.82 = bf16[4,256,768]{2,1,0:T(8,128)(2,1)} fusion(bf16[1,768,3072]{2,1,0:T(8,128)(2,1)} %param.23, bf16[4,1,256,3072]{3,2,0,1:T(8,128)(2,1)S(1)} %fusion.6), kind=kOutput, calls=%fused_computation.96 | convolution fusion | flops 4832624640 | bytes 12582912 | tf_op jit(solution)/shard_map/secf,edf->secd/dot_general | solution.py:238
  284.1 8.2 %fusion.56 = bf16[1,768,3072]{2,1,0:T(8,128)(2,1)} fusion(bf16[4,256,768]{2,1,0:T(8,128)(2,1)} %all-to-all-done, bf16[4,1,256,3072]{3,2,0,1:T(8,128)(2,1)S(1)} %fusion.6), kind=kOutput, calls=%fused_computation.71 | convolution fusion | flops 4834197504 | bytes 12582912 | tf_op jit(solution)/shard_map/secd,secf->edf/dot_general | solution.py:237
  292.3 4.4 all-to-all-done.1
  296.7 4.4 all-to-all-start.3
  301.1 12.0 %fusion.59 = bf16[1,3072,768]{2,1,0:T(8,128)(2,1)} fusion(bf16[4,256,768]{2,1,0:T(8,128)(2,1)} %all-to-all-done.2, f32[4,256,3072]{2,1,0:T(8,128)} %copy-done.64), kind=kOutput, calls=%fused_computation.72 | convolution fusion | flops 4862509056 | bytes 18874368 | tf_op jit(solution)/shard_map/secf,secd->efd/dot_general | solution.py:230
  313.4 4.7 gather_fusion.3
  318.1 19.5 %all-to-all-done.3 = bf16[4,256,768]{2,1,0:T(8,128)(2,1)} async-done(((bf16[4,256,768]{2,1,0:T(8,128)(2,1)}), bf16[4,256,768]{2,1,0:T(8,128)(2,1)}, u32[]{:S(2)}, u32[]{:S(2)}) %all-to-all-start.3) | async-done | bytes 1572896 | tf_op jit(solution)/shard_map/all_to_all | solution.py:241
  337.6 4.7 gather_fusion.5
  342.3 3.1 fusion.102
  345.4 3.7 fusion.100
  356.2 8.6 %fusion.110 = bf16[12,64,512]{2,1,0:T(8,128)(2,1)} fusion(bf16[512,12,64]{0,2,1:T(8,128)(2,1)} %bitcast.311, f32[12,512,512]{1,2,0:T(8,128)} %get-tuple-element.245, f32[12,512]{1,0:T(8,128)} %log_add_fusion, pred[512,512]{0,1:T(8,128)(4,1)} %get-tuple-element.240), kind=kOutput, calls=%fused_computation.132 | convolution fusion | flops 415629312 | bytes 14442496 | tf_op jit(solution)/shard_map/while/body/eval_jaxpr/hqk,qhd->khd/dot_general | solution.py:126
  364.8 7.8 %multiply_convert_fusion = bf16[12,512,512]{1,2,0:T(8,128)(2,1)S(1)} fusion(f32[12,512,512]{1,2,0:T(8,128)} %get-tuple-element.245, f32[12,512]{1,0:T(8,128)S(1)} %bitcast.331, f32[12,512]{1,0:T(8,128)S(1)} %copy-done.47, pred[512,512]{0,1:T(8,128)(4,1)S(1)} %copy-done.22, bf16[512,12,64]{0,2,1:T(8,128)(2,1)S(1)} %bitcast.312, ...), kind=kOutput, calls=%fused_computation.22 | convolution fusion | flops 421527552 | bytes 20758528 | tf_op jit(solution)/shard_map/while/body/eval_jaxpr/qhd,khd->hqk/dot_general | solution.py:96
  372.7 7.6 %multiply_convert_fusion.2 = bf16[12,512,512]{1,2,0:T(8,128)(2,1)S(1)} fusion(f32[12,512,512]{1,2,0:T(8,128)} %get-tuple-element.262, f32[12,512]{1,0:T(8,128)S(1)} %bitcast.332, f32[12,512]{1,0:T(8,128)S(1)} %copy-done.47, pred[512,512]{0,1:T(8,128)(4,1)} %get-tuple-element.239, bf16[512,12,64]{0,2,1:T(8,128)(2,1)S(1)} %bitcast.313, ...), kind=kOutput, calls=%fused_computation.26 | convolution fusion | flops 421527552 | bytes 20758528 | tf_op jit(solution)/shard_map/while/body/eval_jaxpr/qhd,khd->hqk/dot_general | solution.py:96
  380.3 2.4 fusion.160
  382.7 3.1 convolution_multiply_fusion
  385.8 8.0 %multiply_convert_fusion.1 = bf16[12,512,512]{1,2,0:T(8,128)(2,1)S(1)} fusion(f32[12,512,512]{1,2,0:T(8,128)} %get-tuple-element.247, f32[12,512]{1,0:T(8,128)S(1)} %bitcast.333, f32[12,512]{1,0:T(8,128)S(1)} %copy-done.47, pred[512,512]{0,1:T(8,128)(4,1)} %get-tuple-element.241, bf16[512,12,64]{0,2,1:T(8,128)(2,1)S(1)} %bitcast.314, ...), kind=kOutput, calls=%fused_computation.24 | convolution fusion | flops 421527552 | bytes 20758528 | tf_op jit(solution)/shard_map/while/body/eval_jaxpr/qhd,khd->hqk/dot_general | solution.py:96
  398.5 3.1 convolution_multiply_fusion.1
  401.7 2.3 fusion.161
  404.0 6.1 fusion.30
  410.2 3.4 fusion.64
  419.8 3.6 fusion.32
  423.5 14.7 %collective-permute-done.3 = bf16[512,1536]{0,1:T(8,128)(2,1)} collective-permute-done((bf16[512,1536]{0,1:T(8,128)(2,1)}, bf16[512,1536]{0,1:T(8,128)(2,1)}, u32[]{:S(2)}, u32[]{:S(2)}) %collective-permute-start.3) | collective-permute-done | bytes 1572896 | tf_op jit(solution)/shard_map/ppermute | solution.py:17
  441.4 5.3 fusion.106
  446.7 23.3 %all-reduce.8.cloned.1.call-done = (bf16[1,768,3072]{2,1,0:T(8,128)(2,1)}, bf16[1,3072,768]{2,1,0:T(8,128)(2,1)}) async-done(((bf16[1,768,3072]{2,1,0:T(8,128)(2,1)}, bf16[1,3072,768]{2,1,0:T(8,128)(2,1)}), (bf16[1,768,3072]{2,1,0:T(8,128)(2,1)}, bf16[1,3072,768]{2,1,0:T(8,128)(2,1)})) %all-reduce.8.cloned.1.call-update) | async-done | bytes 9437200 | tf_op jit(solution)/shard_map/psum | solution.py:304
  470.0 7.5 %convert_element_type.162 = f32[1,768,3072]{2,1,0:T(8,128)} convert(bf16[1,768,3072]{2,1,0:T(8,128)(2,1)} %get-tuple-element.192) | non-fusion elementwise | flops 2359296 | bytes 14155776 | tf_op jit(solution)/shard_map/convert_element_type | solution.py:304
  477.6 4.5 convert_element_type.165
  482.1 4.2 fusion.96
  486.2 55.8 %all-reduce = (f32[768]{0:T(1024)}, f32[768]{0:T(1024)}, f32[768]{0:T(1024)}, f32[768]{0:T(1024)}) all-reduce(f32[768]{0:T(1024)} %get-tuple-element.167, f32[768]{0:T(1024)} %get-tuple-element.170, f32[768]{0:T(1024)S(1)} %get-tuple-element.165, f32[768]{0:T(1024)S(1)} %copy-done.50), channel_id=1, replica_groups=mesh['seq'=8,'exp'=4] {'seq','exp'}, use_global_device_ids=true, to_apply=%region_23.24 | all-reduce | flops 3072 | bytes 24576 | tf_op jit(solution)/shard_map/psum | solution.py:292
  543.4 4.0 fusion.95
  547.3 129.1 %all-reduce.6.cloned.1.call-done = (f32[768,2304]{1,0:T(8,128)}, f32[768,768]{1,0:T(8,128)}) async-done(((f32[768,2304]{1,0:T(8,128)}, f32[768,768]{1,0:T(8,128)}), (f32[768,2304]{1,0:T(8,128)}, f32[768,768]{1,0:T(8,128)})) %all-reduce.6.cloned.1.call-update) | async-done | bytes 9437200 | tf_op jit(solution)/shard_map/psum | solution.py:292
  676.4 6.6 copy.132
  (207 shorter events, 55.1 us)
Async XLA Ops:
  8.7 4.9 copy-start.48
  10.2 9.6 %copy-start.57 = (s32[1,512]{1,0:T(1,128)S(1)}, s32[1,512]{1,0:T(1,128)}, u32[]{:S(2)}) copy-start(s32[1,512]{1,0:T(1,128)} %param.14) | copy-start | bytes 6148
  16.2 29.7 %collective-permute-start = (bf16[512,1536]{1,0:T(8,128)(2,1)}, bf16[512,1536]{1,0:T(8,128)(2,1)}, u32[]{:S(2)}, u32[]{:S(2)}) collective-permute-start(bf16[512,1536]{1,0:T(8,128)(2,1)} %slice.67), channel_id=1, source_target_pairs={{0,4},{4,8},{8,12},{12,16},{16,20},{20,24},{24,28},{1,5},{5,9},{9,... | collective-permute-start | bytes 4718600 | tf_op jit(solution)/shard_map/ppermute | solution.py:17
  40.5 18.1 %copy-start.44 = (s32[1024]{0:T(1024)}, s32[1024]{0:T(1024)S(1)}, u32[]{:S(2)}) copy-start(s32[1024]{0:T(1024)S(1)} %broadcast_clamp_fusion) | copy-start | bytes 12292
  45.9 44.2 %collective-permute-start.1 = (bf16[512,1536]{1,0:T(8,128)(2,1)}, bf16[512,1536]{1,0:T(8,128)(2,1)}, u32[]{:S(2)}, u32[]{:S(2)}) collective-permute-start(bf16[512,1536]{1,0:T(8,128)(2,1)} %collective-permute-done), channel_id=1, source_target_pairs={{0,4},{4,8},{8,12},{12,16},{16,20},{20,24},{24,28},{1,5},{5,9},{9,... | collective-permute-start | bytes 4718600 | tf_op jit(solution)/shard_map/ppermute | solution.py:17
  97.3 8.1 %copy-start.33 = (f32[12,512]{1,0:T(8,128)S(1)}, f32[12,512]{1,0:T(8,128)}, u32[]{:S(2)}) copy-start(f32[12,512]{1,0:T(8,128)} %get-tuple-element.248) | copy-start | bytes 73732
  97.3 8.1 %copy-start.39 = (f32[12,512]{1,0:T(8,128)S(1)}, f32[12,512]{1,0:T(8,128)}, u32[]{:S(2)}) copy-start(f32[12,512]{1,0:T(8,128)} %get-tuple-element.246) | copy-start | bytes 73732
  97.3 8.8 %copy-start.19 = (pred[512,512]{0,1:T(8,128)(4,1)S(1)}, pred[512,512]{0,1:T(8,128)(4,1)}, u32[]{:S(2)}) copy-start(pred[512,512]{0,1:T(8,128)(4,1)} %get-tuple-element.241) | copy-start | bytes 786436
  105.4 7.9 %copy-start.41 = (f32[12,512]{1,0:T(8,128)}, f32[12,512]{1,0:T(8,128)S(1)}, u32[]{:S(2)}) copy-start(f32[12,512]{1,0:T(8,128)S(1)} %get-tuple-element.244) | copy-start | bytes 73732
  106.1 7.3 %copy-start.38 = (f32[12,512]{1,0:T(8,128)}, f32[12,512]{1,0:T(8,128)S(1)}, u32[]{:S(2)}) copy-start(f32[12,512]{1,0:T(8,128)S(1)} %get-tuple-element.210) | copy-start | bytes 73732
  106.1 28.1 %slice-start = ((s8[12582912]{0:T(1024)(128)(4,1)}), s8[4194304]{0:T(1024)(128)(4,1)S(1)}, s32[]{:S(2)}) async-start(s8[12582912]{0:T(1024)(128)(4,1)} %bitcast.290), calls=%async_computation.6 | async-start | bytes 8388608
  106.1 28.1 %slice-start.1 = ((s8[12582912]{0:T(1024)(128)(4,1)}), s8[4194304]{0:T(1024)(128)(4,1)S(1)}, s32[]{:S(2)}) async-start(s8[12582912]{0:T(1024)(128)(4,1)} %bitcast.290), calls=%async_computation.7 | async-start | bytes 8388608
  113.4 36.4 %copy-start.34 = (f32[12,512]{1,0:T(8,128)}, f32[12,512]{1,0:T(8,128)S(1)}, u32[]{:S(2)}) copy-start(f32[12,512]{1,0:T(8,128)S(1)} %fusion.13) | copy-start | bytes 73732
  113.4 20.8 %slice-start.2 = ((s8[12582912]{0:T(1024)(128)(4,1)}), s8[4194304]{0:T(1024)(128)(4,1)S(1)}, s32[]{:S(2)}) async-start(s8[12582912]{0:T(1024)(128)(4,1)} %bitcast.290), calls=%async_computation.8 | async-start | bytes 8388608
  137.8 12.1 %copy-start.35 = (f32[12,512]{1,0:T(8,128)}, f32[12,512]{1,0:T(8,128)S(1)}, u32[]{:S(2)}) copy-start(f32[12,512]{1,0:T(8,128)S(1)} %fusion.11) | copy-start | bytes 73732
  142.5 7.4 %copy-start.40 = (f32[12,512]{1,0:T(8,128)S(1)}, f32[12,512]{1,0:T(8,128)}, u32[]{:S(2)}) copy-start(f32[12,512]{1,0:T(8,128)} %get-tuple-element.246) | copy-start | bytes 73732
  142.5 7.4 %copy-start.42 = (f32[12,512]{1,0:T(8,128)S(1)}, f32[12,512]{1,0:T(8,128)}, u32[]{:S(2)}) copy-start(f32[12,512]{1,0:T(8,128)} %copy-done.41) | copy-start | bytes 73732
  142.5 7.4 %copy-start.21 = (pred[512,512]{0,1:T(8,128)(4,1)S(1)}, pred[512,512]{0,1:T(8,128)(4,1)}, u32[]{:S(2)}) copy-start(pred[512,512]{0,1:T(8,128)(4,1)} %get-tuple-element.240) | copy-start | bytes 786436
  142.5 7.4 %copy-start.28 = (bf16[512,768]{0,1:T(8,128)(2,1)S(1)}, bf16[512,768]{0,1:T(8,128)(2,1)}, u32[]{:S(2)}) copy-start(bf16[512,768]{0,1:T(8,128)(2,1)} %copy.92) | copy-start | bytes 2359300
  142.5 7.4 %copy-start.37 = (f32[12,512]{1,0:T(8,128)S(1)}, f32[12,512]{1,0:T(8,128)}, u32[]{:S(2)}) copy-start(f32[12,512]{1,0:T(8,128)} %get-tuple-element.196) | copy-start | bytes 73732
  142.5 7.4 %copy-start.62 = (f32[12,64,512]{2,1,0:T(8,128)S(1)}, f32[12,64,512]{2,1,0:T(8,128)}, u32[]{:S(2)}) copy-start(f32[12,64,512]{2,1,0:T(8,128)} %fusion.36) | copy-start | bytes 4718596
  142.5 7.4 %copy-start.63 = (f32[12,64,512]{2,1,0:T(8,128)S(1)}, f32[12,64,512]{2,1,0:T(8,128)}, u32[]{:S(2)}) copy-start(f32[12,64,512]{2,1,0:T(8,128)} %fusion.38) | copy-start | bytes 4718596
  149.9 8.9 %copy-start.36 = (f32[12,512]{1,0:T(8,128)}, f32[12,512]{1,0:T(8,128)S(1)}, u32[]{:S(2)}) copy-start(f32[12,512]{1,0:T(8,128)S(1)} %fusion.15) | copy-start | bytes 73732
  150.0 8.8 %copy-start.10 = (bf16[1,512,768]{2,1,0:T(8,128)(2,1)S(1)}, bf16[1,512,768]{2,1,0:T(8,128)(2,1)}, u32[]{:S(2)}) copy-start(bf16[1,512,768]{2,1,0:T(8,128)(2,1)} %param.13) | copy-start | bytes 2359300
  150.0 8.8 %copy-start.59 = (bf16[768,768]{1,0:T(8,128)(2,1)S(1)}, bf16[768,768]{1,0:T(8,128)(2,1)}, u32[]{:S(2)}) copy-start(bf16[768,768]{1,0:T(8,128)(2,1)} %param.22) | copy-start | bytes 3538948
  173.5 41.0 %all-to-all-start = ((bf16[4,256,768]{2,1,0:T(8,128)(2,1)}), bf16[4,256,768]{2,1,0:T(8,128)(2,1)}, u32[]{:S(2)}, u32[]{:S(2)}) async-start(bf16[4,256,768]{2,1,0:T(8,128)(2,1)} %get-tuple-element.243), calls=%async_computation | async-start | bytes 3145728 | tf_op jit(solution)/shard_map/all_to_all | solution.py:207
  214.5 40.9 %all-to-all-start.2 = ((bf16[4,256,768]{2,1,0:T(8,128)(2,1)}), bf16[4,256,768]{2,1,0:T(8,128)(2,1)}, u32[]{:S(2)}, u32[]{:S(2)}) async-start(bf16[4,256,768]{2,1,0:T(8,128)(2,1)} %get-tuple-element.242), calls=%async_computation.2 | async-start | bytes 3145728 | tf_op jit(solution)/shard_map/all_to_all | solution.py:227
  226.3 4.5 copy-start.64
  255.4 41.3 %all-to-all-start.1 = ((bf16[4,256,768]{2,1,0:T(8,128)(2,1)}), bf16[4,256,768]{2,1,0:T(8,128)(2,1)}, u32[]{:S(2)}, u32[]{:S(2)}) async-start(bf16[4,256,768]{2,1,0:T(8,128)(2,1)} %fusion.77), calls=%async_computation.1 | async-start | bytes 3145728 | tf_op jit(solution)/shard_map/all_to_all | solution.py:215
  296.7 40.9 %all-to-all-start.3 = ((bf16[4,256,768]{2,1,0:T(8,128)(2,1)}), bf16[4,256,768]{2,1,0:T(8,128)(2,1)}, u32[]{:S(2)}, u32[]{:S(2)}) async-start(bf16[4,256,768]{2,1,0:T(8,128)(2,1)} %fusion.82), calls=%async_computation.3 | async-start | bytes 3145728 | tf_op jit(solution)/shard_map/all_to_all | solution.py:241
  301.1 169.0 %all-reduce.8.cloned.1.call-start = ((), (), s32[]{:S(2)}) async-start(), calls=%async_computation.5 | async-start | bytes 18874368 | tf_op jit(solution)/shard_map/psum | solution.py:304
  313.2 363.2 %all-reduce.6.cloned.1.call-start = ((), (), s32[]{:S(2)}) async-start(), calls=%async_computation.4 | async-start | bytes 18874368 | tf_op jit(solution)/shard_map/psum | solution.py:292
  318.1 24.2 %copy-start.46 = (f32[512]{0:T(512)S(1)}, f32[512]{0:T(512)}, u32[]{:S(2)}) copy-start(f32[512]{0:T(512)} %copy-done.45) | copy-start | bytes 6148
  342.3 8.0 %copy-start.60 = (bf16[768,768]{1,0:T(8,128)(2,1)S(1)}, bf16[768,768]{1,0:T(8,128)(2,1)}, u32[]{:S(2)}) copy-start(bf16[768,768]{1,0:T(8,128)(2,1)} %param.22) | copy-start | bytes 3538948
  356.2 8.6 %copy-start.17 = (bf16[512,768]{0,1:T(8,128)(2,1)S(1)}, bf16[512,768]{0,1:T(8,128)(2,1)}, u32[]{:S(2)}) copy-start(bf16[512,768]{0,1:T(8,128)(2,1)} %copy.94) | copy-start | bytes 2359300
  356.2 8.6 %copy-start.22 = (pred[512,512]{0,1:T(8,128)(4,1)S(1)}, pred[512,512]{0,1:T(8,128)(4,1)}, u32[]{:S(2)}) copy-start(pred[512,512]{0,1:T(8,128)(4,1)} %get-tuple-element.240) | copy-start | bytes 786436
  356.2 8.6 %copy-start.29 = (bf16[512,768]{0,1:T(8,128)(2,1)S(1)}, bf16[512,768]{0,1:T(8,128)(2,1)}, u32[]{:S(2)}) copy-start(bf16[512,768]{0,1:T(8,128)(2,1)} %copy.92) | copy-start | bytes 2359300
  356.2 8.6 %copy-start.47 = (f32[12,512]{1,0:T(8,128)S(1)}, f32[12,512]{1,0:T(8,128)}, u32[]{:S(2)}) copy-start(f32[12,512]{1,0:T(8,128)} %log_add_fusion) | copy-start | bytes 73732
  372.7 7.6 %copy-start.8 = (bf16[512,768]{0,1:T(8,128)(2,1)S(1)}, bf16[512,768]{0,1:T(8,128)(2,1)}, u32[]{:S(2)}) copy-start(bf16[512,768]{0,1:T(8,128)(2,1)} %copy.85) | copy-start | bytes 2359300
  397.1 4.6 copy-start.7
  397.1 13.0 %collective-permute-start.2 = (bf16[512,1536]{0,1:T(8,128)(2,1)}, bf16[512,1536]{0,1:T(8,128)(2,1)}, u32[]{:S(2)}, u32[]{:S(2)}) collective-permute-start(bf16[512,1536]{0,1:T(8,128)(2,1)} %pad_maximum_fusion.1), channel_id=1, source_target_pairs={{4,0},{8,4},{12,8},{16,12},{20,16},{24,20},{28,24},{5,1},{9,5},{13... | collective-permute-start | bytes 4718600 | tf_op jit(solution)/shard_map/ppermute | solution.py:17
  404.0 6.1 copy-start.15
  404.0 15.7 %slice-start.3 = ((s8[12582912]{0:T(1024)(128)(4,1)}), s8[4194304]{0:T(1024)(128)(4,1)S(1)}, s32[]{:S(2)}) async-start(s8[12582912]{0:T(1024)(128)(4,1)} %bitcast.292), calls=%async_computation.9 | async-start | bytes 8388608
  404.0 15.7 %slice-start.4 = ((s8[12582912]{0:T(1024)(128)(4,1)}), s8[4194304]{0:T(1024)(128)(4,1)S(1)}, s32[]{:S(2)}) async-start(s8[12582912]{0:T(1024)(128)(4,1)} %bitcast.292), calls=%async_computation.10 | async-start | bytes 8388608
  410.1 5.3 copy-start.4
  410.1 5.3 copy-start.27
  410.2 7.5 %copy-start.5 = (f32[12,64,512]{2,1,0:T(8,128)S(1)}, f32[12,64,512]{2,1,0:T(8,128)}, u32[]{:S(2)}) copy-start(f32[12,64,512]{2,1,0:T(8,128)} %fusion.160) | copy-start | bytes 4718596
  410.2 7.5 %copy-start.6 = (f32[12,64,512]{2,1,0:T(8,128)S(1)}, f32[12,64,512]{2,1,0:T(8,128)}, u32[]{:S(2)}) copy-start(f32[12,64,512]{2,1,0:T(8,128)} %fusion.161) | copy-start | bytes 4718596
  410.2 7.5 %copy-start.9 = (bf16[512,768]{0,1:T(8,128)(2,1)S(1)}, bf16[512,768]{0,1:T(8,128)(2,1)}, u32[]{:S(2)}) copy-start(bf16[512,768]{0,1:T(8,128)(2,1)} %copy.91) | copy-start | bytes 2359300
  413.6 6.1 slice-start.5
  413.6 24.5 %collective-permute-start.3 = (bf16[512,1536]{0,1:T(8,128)(2,1)}, bf16[512,1536]{0,1:T(8,128)(2,1)}, u32[]{:S(2)}, u32[]{:S(2)}) collective-permute-start(bf16[512,1536]{0,1:T(8,128)(2,1)} %fusion.64), channel_id=1, source_target_pairs={{4,0},{8,4},{12,8},{16,12},{20,16},{24,20},{28,24},{5,1},{9,5},{13... | collective-permute-start | bytes 4718600 | tf_op jit(solution)/shard_map/ppermute | solution.py:17
  419.8 18.4 %copy-start.14 = (f32[12,64,512]{2,1,0:T(8,128)S(1)}, f32[12,64,512]{2,1,0:T(8,128)}, u32[]{:S(2)}) copy-start(f32[12,64,512]{2,1,0:T(8,128)} %convolution_multiply_fusion) | copy-start | bytes 4718596
  423.4 17.9 %copy-start.11 = (bf16[1,512,768]{2,1,0:T(8,128)(2,1)S(1)}, bf16[1,512,768]{2,1,0:T(8,128)(2,1)}, u32[]{:S(2)}) copy-start(bf16[1,512,768]{2,1,0:T(8,128)(2,1)} %param.13) | copy-start | bytes 2359300
  423.4 17.9 %copy-start.31 = (bf16[12,64,512]{2,1,0:T(8,128)(2,1)S(1)}, bf16[12,64,512]{2,1,0:T(8,128)(2,1)}, u32[]{:S(2)}) copy-start(bf16[12,64,512]{2,1,0:T(8,128)(2,1)} %multiply_convert_fusion.4) | copy-start | bytes 2359300
  423.4 17.9 %copy-start.49 = (f32[512]{0:T(512)S(1)}, f32[512]{0:T(512)}, u32[]{:S(2)}) copy-start(f32[512]{0:T(512)} %copy-done.48) | copy-start | bytes 6148
  423.4 17.9 %copy-start.52 = (f32[512]{0:T(512)S(1)}, f32[512]{0:T(512)}, u32[]{:S(2)}) copy-start(f32[512]{0:T(512)} %copy-done.51) | copy-start | bytes 6148
  423.4 17.9 %copy-start.54 = (f32[768]{0:T(1024)S(1)}, f32[768]{0:T(1024)}, u32[]{:S(2)}) copy-start(f32[768]{0:T(1024)} %param.17) | copy-start | bytes 9220
  423.4 17.9 %copy-start.61 = (f32[768]{0:T(1024)S(1)}, f32[768]{0:T(1024)}, u32[]{:S(2)}) copy-start(f32[768]{0:T(1024)} %param.18) | copy-start | bytes 9220
  470.0 7.5 %copy-start.16 = (bf16[1,3072,768]{2,1,0:T(8,128)(2,1)S(1)}, bf16[1,3072,768]{2,1,0:T(8,128)(2,1)}, u32[]{:S(2)}) copy-start(bf16[1,3072,768]{2,1,0:T(8,128)(2,1)} %get-tuple-element.193) | copy-start | bytes 14155780
  477.5 4.5 copy-start.12
  477.5 4.5 copy-start.25
  477.5 4.5 copy-start.32
  477.5 4.5 copy-start.55
  676.4 6.6 copy-start.23
  (17 other events, 36.6 us)
Sparse Core Ops, SparseCore 0:
  313.3 156.6 all-reduce.7
  477.5 198.8 all-reduce.5
where the time goes:
time: 699 us; the launch traced here: 692 us
  waiting for transfers between devices  233 us (33%)
  matrix products  196 us (28%)
  local copies, waits for them, and re-layouts  86.4 us (12%)
  other arithmetic  74.9 us (11%)
  blocking collectives  55.8 us (8%)
  starting transfers between devices  29.9 us (4%)
  between operations  15.3 us (2%)
    psum x1, waiting for transfers between devices, on_device(): lax.psum((grad_w_qkv, grad_w_out, grad_first_gain, grad_first_bias, grad_...  129 us
    psum x1, blocking collectives, on_device(): lax.psum((grad_w_qkv, grad_w_out, grad_first_gain, grad_first_bias, grad_...  55.8 us
    dot_general x3, matrix products, step(): jnp.einsum('hqk,khd->qhd', shares.astype(jnp.bfloat16), value_rows, prefe...  34.3 us
    all_to_all x1, waiting for transfers between devices, on_device(): lax.all_to_all(send, 'exp', split_axis=0, concat_axis=0, tiled=True)  28.2 us
    dot_general x3, matrix products, step(): jnp.einsum('qhd,khd->hqk', queries, key_rows, preferred_element_type=jnp....  25.3 us
    dot_general x3, matrix products, backward_core(): jnp.einsum('qhd,khd->hqk', grad_heads, value_rows, preferred_element_type...  23.4 us
    psum x1, waiting for transfers between devices, on_device(): lax.psum(grad_w_up.astype(jnp.bfloat16), 'seq').astype(jnp.float32)  23.3 us
    all_to_all x1, waiting for transfers between devices, on_device(): lax.all_to_all(grad_slots.reshape(experts_total, capacity, width), 'exp',...  19.5 us
  transfers between devices with their start and end apart: 10, of which 7 were waited for; matrix products, arithmetic and copies ran while one was open for 36% of the time, Pallas kernels for 0%

commit v1 on v0

--- a/solution.py
+++ b/solution.py
@@ -301,7 +301,9 @@
         ("seq", "exp"),
     )
     expert_sums = (
-        lax.psum(grad_w_up.astype(jnp.bfloat16), "seq").astype(jnp.float32),
+        jnp.sum(lax.all_gather(grad_w_up.astype(jnp.bfloat16), axis_name="seq"), 0).astype(
+            jnp.float32
+        ),
         lax.psum(grad_w_down.astype(jnp.bfloat16), "seq").astype(jnp.float32),
     )
     return (

time: 699 us -> 773 us (1.11)
  blocking collectives: 55.8 us -> 130 us
  other arithmetic: 74.9 us -> 94.1 us
  matrix products: 196 us -> 186 us
    all_to_all x0 -> x1, blocking collectives: none -> 40.8 us  [on_device(): lax.all_to_all(send, 'exp', split_axis=0, concat_axis=0, tiled=True)]
    psum x1, blocking collectives: 55.8 us -> 88.8 us  [on_device(): lax.psum((grad_w_qkv, grad_w_out, grad_first_gain, grad_first_bias, grad_...]
    all_to_all x1 -> x0, waiting for transfers between devices: 28.2 us -> none  [on_device(): lax.all_to_all(send, 'exp', split_axis=0, concat_axis=0, tiled=True)]
    psum x1, waiting for transfers between devices: 23.3 us -> 0.02 us  [on_device(): lax.psum(grad_w_down.astype(jnp.bfloat16), 'seq').astype(jnp.float32)]
    all_to_all x1, waiting for transfers between devices: 4.43 us -> 23.6 us  [on_device(): lax.all_to_all(expert_out.reshape(experts_total, capacity, width), 'exp',...]
    psum x1, waiting for transfers between devices: 129 us -> 146 us  [on_device(): lax.psum((grad_w_qkv, grad_w_out, grad_first_gain, grad_first_bias, grad_...]
    reduce_sum x0 -> x1, other arithmetic: none -> 16.5 us  [on_device(): jnp.sum(lax.all_gather(grad_w_up.astype(jnp.bfloat16), axis_name='seq'), 0)]
    all_to_all x1, waiting for transfers between devices: 13.9 us -> 26.1 us  [on_device(): lax.all_to_all(grad_send, 'exp', split_axis=0, concat_axis=0, tiled=True)]
  transfers between devices with their start and end apart: 10 -> 10, of which waited for: 7 -> 5; matrix products, arithmetic and copies ran while one was open for 36% -> 34% of each run, Pallas kernels for 0% -> 0%
where the time goes in v1:
time: 773 us; the launch traced here: 767 us
  waiting for transfers between devices  231 us (30%)
  matrix products  186 us (24%)
  blocking collectives  130 us (17%)
  other arithmetic  94.1 us (12%)
  local copies, waits for them, and re-layouts  85 us (11%)
  starting transfers between devices  25.1 us (3%)
  between operations  15.1 us (2%)
    psum x1, waiting for transfers between devices, on_device(): lax.psum((grad_w_qkv, grad_w_out, grad_first_gain, grad_first_bias, grad_...  146 us
    psum x1, blocking collectives, on_device(): lax.psum((grad_w_qkv, grad_w_out, grad_first_gain, grad_first_bias, grad_...  88.8 us
    all_to_all x1, blocking collectives, on_device(): lax.all_to_all(send, 'exp', split_axis=0, concat_axis=0, tiled=True)  40.8 us
    all_to_all x1, waiting for transfers between devices, on_device(): lax.all_to_all(grad_send, 'exp', split_axis=0, concat_axis=0, tiled=True)  26.1 us
    dot_general x3, matrix products, step(): jnp.einsum('qhd,khd->hqk', queries, key_rows, preferred_element_type=jnp....  25.1 us
    dot_general x3, matrix products, backward_core(): jnp.einsum('qhd,khd->hqk', grad_heads, value_rows, preferred_element_type...  23.8 us
    all_to_all x1, waiting for transfers between devices, on_device(): lax.all_to_all(expert_out.reshape(experts_total, capacity, width), 'exp',...  23.6 us
    all_to_all x1, waiting for transfers between devices, on_device(): lax.all_to_all(grad_slots.reshape(experts_total, capacity, width), 'exp',...  23.6 us
  transfers between devices with their start and end apart: 10, of which 5 were waited for; matrix products, arithmetic and copies ran while one was open for 34% of the time, Pallas kernels for 0%

profile of v1, /device:TPU:0, one launch (start us, length us, event | category | flops | bytes accessed | tf_op | source)
XLA Modules:
  0.0 766.6 jit_solution(8098123838812625864)
XLA Ops:
  10.2 3.3 convolution_convert_fusion
  16.2 3.5 collective-permute-start
  19.7 3.4 gather_fusion
  23.3 3.8 sort.31
  29.1 11.3 %gather_fusion.1 = s32[1024]{0:T(1024)} fusion(s32[512]{0:T(512)S(1)} %get-tuple-element.163, s32[1024]{0:T(1024)S(1)} %broadcast_clamp_fusion.1), kind=kCustom, calls=%fused_computation.1 | custom fusion | bytes 12288 | tf_op jit(solution)/shard_map/gather | solution.py:202
  41.9 3.1 fusion.152
  47.2 4.5 collective-permute-start.1
  53.0 2.3 copy.84
  55.3 2.3 copy.85
  60.0 7.3 gather_fusion.4
  67.3 8.5 %select_reduce_fusion.2 = (f32[12,512]{1,0:T(8,128)}, f32[12,512,512]{1,2,0:T(8,128)}) fusion(pred[512,512]{0,1:T(8,128)(4,1)} %get-tuple-element.237, bf16[512,12,64]{0,2,1:T(8,128)(2,1)} %bitcast.292, bf16[512,12,64]{0,2,1:T(8,128)(2,1)} %bitcast.299), kind=kOutput, calls=%fused_computation.33 | convolution fusion | flops 412084224 | bytes 14442496 | tf_op jit(solution)/shard_map/while/body/eval_jaxpr/qhd,khd->hqk/dot_general | solution.py:71
  75.8 2.6 fusion.154
  83.0 8.5 %select_reduce_fusion.1 = (f32[12,512]{1,0:T(8,128)}, f32[12,512,512]{1,2,0:T(8,128)}) fusion(pred[512,512]{0,1:T(8,128)(4,1)} %get-tuple-element.239, bf16[512,12,64]{0,2,1:T(8,128)(2,1)} %bitcast.293, bf16[512,12,64]{0,2,1:T(8,128)(2,1)} %bitcast.301), kind=kOutput, calls=%fused_computation.31 | convolution fusion | flops 412084224 | bytes 14442496 | tf_op jit(solution)/shard_map/while/body/eval_jaxpr/qhd,khd->hqk/dot_general | solution.py:71
  91.5 2.6 fusion.153
  94.1 2.3 copy.91
  98.8 8.0 %select_reduce_fusion = (f32[12,512]{1,0:T(8,128)S(1)}, f32[12,512,512]{1,2,0:T(8,128)}) fusion(pred[512,512]{0,1:T(8,128)(4,1)} %get-tuple-element.238, bf16[512,12,64]{0,2,1:T(8,128)(2,1)} %bitcast.294, bf16[512,12,64]{0,2,1:T(8,128)(2,1)} %bitcast.303), kind=kOutput, calls=%fused_computation.29 | convolution fusion | flops 412084224 | bytes 14442496 | tf_op jit(solution)/shard_map/while/body/eval_jaxpr/qhd,khd->hqk/dot_general | solution.py:71
  107.4 7.3 fusion.13
  114.7 8.7 %fusion.36 = f32[12,64,512]{2,1,0:T(8,128)} fusion(bf16[512,12,64]{0,2,1:T(8,128)(2,1)} %bitcast.323, f32[12,512,512]{1,2,0:T(8,128)} %get-tuple-element.245, f32[12,512]{1,0:T(8,128)S(1)} %get-tuple-element.195, pred[512,512]{0,1:T(8,128)(4,1)} %get-tuple-element.239), kind=kOutput, calls=%fused_computation.57 | convolution fusion | flops 415236096 | bytes 15228928 | tf_op jit(solution)/shard_map/while/body/eval_jaxpr/hqk,khd->qhd/dot_general | solution.py:78
  123.5 3.5 fusion.11
  127.0 4.7 fusion.38
  131.8 7.3 fusion.15
  139.3 8.8 %fusion.155 = (bf16[512,12,64]{0,2,1:T(8,128)(2,1)S(1)}, f32[512,12,64]{0,2,1:T(8,128)}) fusion(f32[512,12]{0,1:T(8,128)S(1)} %get-tuple-element.192, bf16[512,12,64]{0,2,1:T(8,128)(2,1)S(1)} %bitcast.326, f32[12,512,512]{1,2,0:T(8,128)} %get-tuple-element.243, f32[12,512]{1,0:T(8,128)S(1)} %copy-done.34, pred[512,512]{0,1:T(8,128)(4,1)S(1)} %copy-done.19, ...), kind=kOutput, calls=%fused_computation.216 | convolution fusion | flops 417988608 | bytes 19259392 | tf_op jit(solution)/shard_map/while/body/eval_jaxpr/hqk,khd->qhd/dot_general | solution.py:78
  151.9 7.0 gather_fusion.2
  158.9 3.3 broadcast_select_fusion
  162.3 40.8 %all_to_all.20 = bf16[4,256,768]{2,1,0:T(8,128)(2,1)} all-to-all(bf16[4,256,768]{2,1,0:T(8,128)(2,1)S(1)} %get-tuple-element.241), channel_id=1, replica_groups=mesh['seq'=8,'exp'=4] {'exp'}, dimensions={0} | all-to-all | bytes 3145728 | tf_op jit(solution)/shard_map/all_to_all | solution.py:207
  203.1 4.4 all-to-all-start.2
  207.5 10.0 %fusion.54 = f32[4,256,3072]{2,1,0:T(8,128)} fusion(bf16[4,256,768]{2,1,0:T(8,128)(2,1)} %all_to_all.20, bf16[1,768,3072]{2,1,0:T(8,128)(2,1)} %param.23), kind=kOutput, calls=%fused_computation.70 | convolution fusion | flops 4831838208 | bytes 18874368 | tf_op jit(solution)/shard_map/secd,edf->secf/dot_general | solution.py:209
  217.5 26.1 %all-to-all-done.2 = bf16[4,256,768]{2,1,0:T(8,128)(2,1)} async-done(((bf16[4,256,768]{2,1,0:T(8,128)(2,1)}), bf16[4,256,768]{2,1,0:T(8,128)(2,1)}, u32[]{:S(2)}, u32[]{:S(2)}) %all-to-all-start.2) | async-done | bytes 1572896 | tf_op jit(solution)/shard_map/all_to_all | solution.py:227
  243.6 12.0 %fusion.56 = bf16[1,3072,768]{2,1,0:T(8,128)(2,1)} fusion(bf16[4,256,768]{2,1,0:T(8,128)(2,1)} %all-to-all-done.2, f32[4,256,3072]{2,1,0:T(8,128)} %fusion.54), kind=kOutput, calls=%fused_computation.72 | convolution fusion | flops 4862509056 | bytes 18874368 | tf_op jit(solution)/shard_map/secf,secd->efd/dot_general | solution.py:230
  256.1 15.8 %fusion.6 = bf16[4,1,256,3072]{3,2,0,1:T(8,128)(2,1)S(1)} fusion(f32[4,256,3072]{2,1,0:T(8,128)} %fusion.54, bf16[4,256,768]{2,1,0:T(8,128)(2,1)} %all-to-all-done.2, bf16[1,3072,768]{2,1,0:T(8,128)(2,1)} %param.24), kind=kOutput, calls=%fused_computation.14 | convolution fusion | flops 4894752768 | bytes 25165824 | tf_op jit(solution)/shard_map/secd,efd->secf/dot_general | solution.py:233
  271.9 2.7 copy-done.61
  274.6 6.8 bitcast_convert_fusion.1
  281.5 9.6 %fusion.79 = bf16[4,256,768]{2,1,0:T(8,128)(2,1)} fusion(bf16[1,768,3072]{2,1,0:T(8,128)(2,1)} %param.23, bf16[4,1,256,3072]{3,2,0,1:T(8,128)(2,1)} %copy-done.61), kind=kOutput, calls=%fused_computation.96 | convolution fusion | flops 4832624640 | bytes 12582912 | tf_op jit(solution)/shard_map/secf,edf->secd/dot_general | solution.py:238
  291.0 4.3 all-to-all-start.3
  295.4 12.6 %fusion.74 = bf16[4,256,768]{2,1,0:T(8,128)(2,1)} fusion(bf16[1,3072,768]{2,1,0:T(8,128)(2,1)} %param.24, f32[4,256,3072]{2,1,0:T(8,128)} %fusion.54), kind=kOutput, calls=%fused_computation.95 | convolution fusion | flops 4860936192 | bytes 18874368 | tf_op jit(solution)/shard_map/secf,efd->secd/dot_general | solution.py:212
  308.0 23.6 %all-to-all-done.3 = bf16[4,256,768]{2,1,0:T(8,128)(2,1)} async-done(((bf16[4,256,768]{2,1,0:T(8,128)(2,1)}), bf16[4,256,768]{2,1,0:T(8,128)(2,1)}, u32[]{:S(2)}, u32[]{:S(2)}) %all-to-all-start.3) | async-done | bytes 1572896 | tf_op jit(solution)/shard_map/all_to_all | solution.py:241
  331.6 4.4 all-to-all-start.1
  336.8 4.4 sort.32
  344.2 4.7 gather_fusion.5
  348.9 23.6 %all-to-all-done.1 = bf16[4,256,768]{2,1,0:T(8,128)(2,1)} async-done(((bf16[4,256,768]{2,1,0:T(8,128)(2,1)}), bf16[4,256,768]{2,1,0:T(8,128)(2,1)}, u32[]{:S(2)}, u32[]{:S(2)}) %all-to-all-start.1) | async-done | bytes 1572896 | tf_op jit(solution)/shard_map/all_to_all | solution.py:215
  372.5 4.7 gather_fusion.3
  377.2 3.1 fusion.99
  380.3 3.6 fusion.97
  390.9 9.3 %multiply_convert_fusion = bf16[12,512,512]{1,2,0:T(8,128)(2,1)S(1)} fusion(f32[12,512,512]{1,2,0:T(8,128)} %get-tuple-element.243, f32[12,512]{1,0:T(8,128)S(1)} %bitcast.330, f32[12,512]{1,0:T(8,128)} %log_add_fusion, pred[512,512]{0,1:T(8,128)(4,1)} %get-tuple-element.238, bf16[512,12,64]{0,2,1:T(8,128)(2,1)} %bitcast.310, bf16[512,12,64]{0,2,1:T(8,128)(2,1)} %bitcast.325), kind=kOutput, calls=%fused_computation.22 | convolution fusion | flops 421527552 | bytes 20758528 | tf_op jit(solution)/shard_map/while/body/eval_jaxpr/qhd,khd->hqk/dot_general | solution.py:96
  402.2 6.1 fusion.107
  411.1 7.3 multiply_convert_fusion.2
  418.4 3.1 convolution_multiply_fusion
  421.5 2.3 fusion.157
  423.9 7.3 multiply_convert_fusion.1
  431.1 3.1 convolution_multiply_fusion.1
  434.3 2.4 fusion.158
  436.7 6.1 fusion.30
  442.9 3.4 fusion.61
  452.5 3.6 fusion.32
  456.1 11.7 %collective-permute-done.3 = bf16[512,1536]{0,1:T(8,128)(2,1)} collective-permute-done((bf16[512,1536]{0,1:T(8,128)(2,1)}, bf16[512,1536]{0,1:T(8,128)(2,1)}, u32[]{:S(2)}, u32[]{:S(2)}) %collective-permute-start.3) | collective-permute-done | bytes 1572896 | tf_op jit(solution)/shard_map/ppermute | solution.py:17
  471.0 5.3 fusion.103
  476.4 7.0 convert_element_type.176
  483.4 4.2 fusion.93
  487.6 88.8 %all-reduce = (f32[768]{0:T(1024)}, f32[768]{0:T(1024)}, f32[768]{0:T(1024)}, f32[768]{0:T(1024)}) all-reduce(f32[768]{0:T(1024)} %get-tuple-element.167, f32[768]{0:T(1024)} %get-tuple-element.170, f32[768]{0:T(1024)S(1)} %get-tuple-element.165, f32[768]{0:T(1024)S(1)} %copy-done.47), channel_id=1, replica_groups=mesh['seq'=8,'exp'=4] {'seq','exp'}, use_global_device_ids=true, to_apply=%region_23.24 | all-reduce | flops 3072 | bytes 24576 | tf_op jit(solution)/shard_map/psum | solution.py:292
  577.7 3.9 fusion.92
  581.6 16.5 %reduce.3 = bf16[768,3072]{1,0:T(8,128)(2,1)} reduce(bf16[8,768,3072]{2,1,0:T(8,128)(2,1)} %bitcast.298, bf16[]{:T(256)} %constant.135.clone.1), dimensions={0}, to_apply=%region_30.31 | reduce | flops 16515072 | bytes 42467328 | tf_op jit(solution)/shard_map/reduce_sum | solution.py:304
  598.1 7.4 bitcast_convert_fusion.2
  605.5 146.1 %all-reduce.7.cloned.1.call-done = (f32[768,2304]{1,0:T(8,128)}, f32[768,768]{1,0:T(8,128)}) async-done(((f32[768,2304]{1,0:T(8,128)}, f32[768,768]{1,0:T(8,128)}), (f32[768,2304]{1,0:T(8,128)}, f32[768,768]{1,0:T(8,128)})) %all-reduce.7.cloned.1.call-update) | async-done | bytes 9437200 | tf_op jit(solution)/shard_map/psum | solution.py:292
  751.6 6.6 copy.131
  (204 shorter events, 54.7 us)
Async XLA Ops:
  7.2 3.0 copy-start
  8.7 4.9 copy-start.45
  10.2 3.3 copy-start.48
  10.2 9.5 %copy-start.54 = (s32[1,512]{1,0:T(1,128)S(1)}, s32[1,512]{1,0:T(1,128)}, u32[]{:S(2)}) copy-start(s32[1,512]{1,0:T(1,128)} %param.14) | copy-start | bytes 6148
  16.2 31.0 %collective-permute-start = (bf16[512,1536]{1,0:T(8,128)(2,1)}, bf16[512,1536]{1,0:T(8,128)(2,1)}, u32[]{:S(2)}, u32[]{:S(2)}) collective-permute-start(bf16[512,1536]{1,0:T(8,128)(2,1)} %slice.67), channel_id=1, source_target_pairs={{0,4},{4,8},{8,12},{12,16},{16,20},{20,24},{24,28},{1,5},{5,9},{9,... | collective-permute-start | bytes 4718600 | tf_op jit(solution)/shard_map/ppermute | solution.py:17
  23.3 5.8 copy-start.55
  41.9 18.1 %copy-start.41 = (s32[1024]{0:T(1024)}, s32[1024]{0:T(1024)S(1)}, u32[]{:S(2)}) copy-start(s32[1024]{0:T(1024)S(1)} %broadcast_clamp_fusion) | copy-start | bytes 12292
  47.2 44.3 %collective-permute-start.1 = (bf16[512,1536]{1,0:T(8,128)(2,1)}, bf16[512,1536]{1,0:T(8,128)(2,1)}, u32[]{:S(2)}, u32[]{:S(2)}) collective-permute-start(bf16[512,1536]{1,0:T(8,128)(2,1)} %collective-permute-done), channel_id=1, source_target_pairs={{0,4},{4,8},{8,12},{12,16},{16,20},{20,24},{24,28},{1,5},{5,9},{9,... | collective-permute-start | bytes 4718600 | tf_op jit(solution)/shard_map/ppermute | solution.py:17
  98.8 8.0 %copy-start.30 = (f32[12,512]{1,0:T(8,128)S(1)}, f32[12,512]{1,0:T(8,128)}, u32[]{:S(2)}) copy-start(f32[12,512]{1,0:T(8,128)} %get-tuple-element.246) | copy-start | bytes 73732
  98.8 8.0 %copy-start.36 = (f32[12,512]{1,0:T(8,128)S(1)}, f32[12,512]{1,0:T(8,128)}, u32[]{:S(2)}) copy-start(f32[12,512]{1,0:T(8,128)} %get-tuple-element.244) | copy-start | bytes 73732
  98.8 8.6 %copy-start.17 = (pred[512,512]{0,1:T(8,128)(4,1)S(1)}, pred[512,512]{0,1:T(8,128)(4,1)}, u32[]{:S(2)}) copy-start(pred[512,512]{0,1:T(8,128)(4,1)} %get-tuple-element.239) | copy-start | bytes 786436
  106.8 7.9 %copy-start.38 = (f32[12,512]{1,0:T(8,128)}, f32[12,512]{1,0:T(8,128)S(1)}, u32[]{:S(2)}) copy-start(f32[12,512]{1,0:T(8,128)S(1)} %get-tuple-element.242) | copy-start | bytes 73732
  107.4 7.3 copy-start.35
  107.4 16.1 %slice-start = ((s8[12582912]{0:T(1024)(128)(4,1)}), s8[4194304]{0:T(1024)(128)(4,1)S(1)}, s32[]{:S(2)}) async-start(s8[12582912]{0:T(1024)(128)(4,1)} %bitcast.288), calls=%async_computation.7 | async-start | bytes 8388608
  107.4 16.1 %slice-start.1 = ((s8[12582912]{0:T(1024)(128)(4,1)}), s8[4194304]{0:T(1024)(128)(4,1)S(1)}, s32[]{:S(2)}) async-start(s8[12582912]{0:T(1024)(128)(4,1)} %bitcast.288), calls=%async_computation.8 | async-start | bytes 8388608
  114.7 24.4 %copy-start.31 = (f32[12,512]{1,0:T(8,128)}, f32[12,512]{1,0:T(8,128)S(1)}, u32[]{:S(2)}) copy-start(f32[12,512]{1,0:T(8,128)S(1)} %fusion.13) | copy-start | bytes 73732
  114.7 8.7 %slice-start.2 = ((s8[12582912]{0:T(1024)(128)(4,1)}), s8[4194304]{0:T(1024)(128)(4,1)S(1)}, s32[]{:S(2)}) async-start(s8[12582912]{0:T(1024)(128)(4,1)} %bitcast.288), calls=%async_computation.9 | async-start | bytes 8388608
  127.0 12.1 %copy-start.32 = (f32[12,512]{1,0:T(8,128)}, f32[12,512]{1,0:T(8,128)S(1)}, u32[]{:S(2)}) copy-start(f32[12,512]{1,0:T(8,128)S(1)} %fusion.11) | copy-start | bytes 73732
  131.8 7.4 copy-start.37
  131.8 7.4 copy-start.39
  131.8 7.4 copy-start.19
  131.8 7.4 copy-start.27
  131.8 7.4 copy-start.34
  131.8 7.4 copy-start.59
  131.8 7.4 copy-start.60
  139.2 8.9 %copy-start.33 = (f32[12,512]{1,0:T(8,128)}, f32[12,512]{1,0:T(8,128)S(1)}, u32[]{:S(2)}) copy-start(f32[12,512]{1,0:T(8,128)S(1)} %fusion.15) | copy-start | bytes 73732
  139.2 8.8 %copy-start.10 = (bf16[1,512,768]{2,1,0:T(8,128)(2,1)S(1)}, bf16[1,512,768]{2,1,0:T(8,128)(2,1)}, u32[]{:S(2)}) copy-start(bf16[1,512,768]{2,1,0:T(8,128)(2,1)} %param.13) | copy-start | bytes 2359300
  139.3 8.8 %copy-start.56 = (bf16[768,768]{1,0:T(8,128)(2,1)S(1)}, bf16[768,768]{1,0:T(8,128)(2,1)}, u32[]{:S(2)}) copy-start(bf16[768,768]{1,0:T(8,128)(2,1)} %param.22) | copy-start | bytes 3538948
  203.1 40.5 %all-to-all-start.2 = ((bf16[4,256,768]{2,1,0:T(8,128)(2,1)}), bf16[4,256,768]{2,1,0:T(8,128)(2,1)}, u32[]{:S(2)}, u32[]{:S(2)}) async-start(bf16[4,256,768]{2,1,0:T(8,128)(2,1)} %get-tuple-element.240), calls=%async_computation.2 | async-start | bytes 3145728 | tf_op jit(solution)/shard_map/all_to_all | solution.py:227
  207.4 268.9 %all-reduce.5.cloned.1.call-start = ((), (), s32[]{:S(2)}) async-start(), calls=%async_computation.4 | async-start | bytes 9437184 | tf_op jit(solution)/shard_map/psum | solution.py:307
  255.6 326.0 %all-gather.3.cloned.1.call-start = ((), (), s32[]{:S(2)}) async-start(), calls=%async_computation.5 | async-start | bytes 42467328 | tf_op jit(solution)/shard_map/all_gather | solution.py:304
  256.1 18.6 %copy-start.22 = (bf16[4,256,768]{2,1,0:T(8,128)(2,1)S(1)}, bf16[4,256,768]{2,1,0:T(8,128)(2,1)}, u32[]{:S(2)}) copy-start(bf16[4,256,768]{2,1,0:T(8,128)(2,1)} %all_to_all.20) | copy-start | bytes 4718596
  291.0 40.6 %all-to-all-start.3 = ((bf16[4,256,768]{2,1,0:T(8,128)(2,1)}), bf16[4,256,768]{2,1,0:T(8,128)(2,1)}, u32[]{:S(2)}, u32[]{:S(2)}) async-start(bf16[4,256,768]{2,1,0:T(8,128)(2,1)} %fusion.79), calls=%async_computation.3 | async-start | bytes 3145728 | tf_op jit(solution)/shard_map/all_to_all | solution.py:241
  331.6 40.9 %all-to-all-start.1 = ((bf16[4,256,768]{2,1,0:T(8,128)(2,1)}), bf16[4,256,768]{2,1,0:T(8,128)(2,1)}, u32[]{:S(2)}, u32[]{:S(2)}) async-start(bf16[4,256,768]{2,1,0:T(8,128)(2,1)} %fusion.74), calls=%async_computation.1 | async-start | bytes 3145728 | tf_op jit(solution)/shard_map/all_to_all | solution.py:215
  336.0 415.6 %all-reduce.7.cloned.1.call-start = ((), (), s32[]{:S(2)}) async-start(), calls=%async_computation.6 | async-start | bytes 18874368 | tf_op jit(solution)/shard_map/psum | solution.py:292
  348.9 28.3 %copy-start.43 = (f32[512]{0:T(512)S(1)}, f32[512]{0:T(512)}, u32[]{:S(2)}) copy-start(f32[512]{0:T(512)} %copy-done.42) | copy-start | bytes 6148
  377.2 7.8 %copy-start.57 = (bf16[768,768]{1,0:T(8,128)(2,1)S(1)}, bf16[768,768]{1,0:T(8,128)(2,1)}, u32[]{:S(2)}) copy-start(bf16[768,768]{1,0:T(8,128)(2,1)} %param.22) | copy-start | bytes 3538948
  390.9 9.3 %copy-start.1 = (bf16[512,768]{0,1:T(8,128)(2,1)S(1)}, bf16[512,768]{0,1:T(8,128)(2,1)}, u32[]{:S(2)}) copy-start(bf16[512,768]{0,1:T(8,128)(2,1)} %copy.84) | copy-start | bytes 2359300
  409.6 33.2 %collective-permute-start.2 = (bf16[512,1536]{0,1:T(8,128)(2,1)}, bf16[512,1536]{0,1:T(8,128)(2,1)}, u32[]{:S(2)}, u32[]{:S(2)}) collective-permute-start(bf16[512,1536]{0,1:T(8,128)(2,1)} %pad_maximum_fusion.1), channel_id=1, source_target_pairs={{4,0},{8,4},{12,8},{16,12},{20,16},{24,20},{28,24},{5,1},{9,5},{13... | collective-permute-start | bytes 4718600 | tf_op jit(solution)/shard_map/ppermute | solution.py:17
  418.4 3.2 copy-start.7
  431.1 3.2 copy-start.8
  436.7 6.1 copy-start.15
  436.7 15.8 %slice-start.3 = ((s8[12582912]{0:T(1024)(128)(4,1)}), s8[4194304]{0:T(1024)(128)(4,1)S(1)}, s32[]{:S(2)}) async-start(s8[12582912]{0:T(1024)(128)(4,1)} %bitcast.290), calls=%async_computation.10 | async-start | bytes 8388608
  436.7 15.8 %slice-start.4 = ((s8[12582912]{0:T(1024)(128)(4,1)}), s8[4194304]{0:T(1024)(128)(4,1)S(1)}, s32[]{:S(2)}) async-start(s8[12582912]{0:T(1024)(128)(4,1)} %bitcast.290), calls=%async_computation.11 | async-start | bytes 8388608
  442.8 5.3 copy-start.4
  442.8 5.3 copy-start.26
  442.8 7.5 copy-start.5
  442.8 7.4 copy-start.6
  442.8 7.4 copy-start.9
  446.3 6.2 slice-start.5
  446.3 21.6 %collective-permute-start.3 = (bf16[512,1536]{0,1:T(8,128)(2,1)}, bf16[512,1536]{0,1:T(8,128)(2,1)}, u32[]{:S(2)}, u32[]{:S(2)}) collective-permute-start(bf16[512,1536]{0,1:T(8,128)(2,1)} %fusion.61), channel_id=1, source_target_pairs={{4,0},{8,4},{12,8},{16,12},{20,16},{24,20},{28,24},{5,1},{9,5},{13... | collective-permute-start | bytes 4718600 | tf_op jit(solution)/shard_map/ppermute | solution.py:17
  452.4 15.4 %copy-start.14 = (f32[12,64,512]{2,1,0:T(8,128)S(1)}, f32[12,64,512]{2,1,0:T(8,128)}, u32[]{:S(2)}) copy-start(f32[12,64,512]{2,1,0:T(8,128)} %convolution_multiply_fusion) | copy-start | bytes 4718596
  456.1 14.9 %copy-start.11 = (bf16[1,512,768]{2,1,0:T(8,128)(2,1)S(1)}, bf16[1,512,768]{2,1,0:T(8,128)(2,1)}, u32[]{:S(2)}) copy-start(bf16[1,512,768]{2,1,0:T(8,128)(2,1)} %param.13) | copy-start | bytes 2359300
  456.1 14.9 %copy-start.28 = (bf16[12,64,512]{2,1,0:T(8,128)(2,1)S(1)}, bf16[12,64,512]{2,1,0:T(8,128)(2,1)}, u32[]{:S(2)}) copy-start(bf16[12,64,512]{2,1,0:T(8,128)(2,1)} %multiply_convert_fusion.4) | copy-start | bytes 2359300
  456.1 14.9 %copy-start.46 = (f32[512]{0:T(512)S(1)}, f32[512]{0:T(512)}, u32[]{:S(2)}) copy-start(f32[512]{0:T(512)} %copy-done.45) | copy-start | bytes 6148
  456.1 14.9 %copy-start.49 = (f32[512]{0:T(512)S(1)}, f32[512]{0:T(512)}, u32[]{:S(2)}) copy-start(f32[512]{0:T(512)} %copy-done.48) | copy-start | bytes 6148
  456.1 14.9 %copy-start.51 = (f32[768]{0:T(1024)S(1)}, f32[768]{0:T(1024)}, u32[]{:S(2)}) copy-start(f32[768]{0:T(1024)} %param.17) | copy-start | bytes 9220
  456.1 14.9 %copy-start.58 = (f32[768]{0:T(1024)S(1)}, f32[768]{0:T(1024)}, u32[]{:S(2)}) copy-start(f32[768]{0:T(1024)} %param.18) | copy-start | bytes 9220
  476.3 7.0 copy-start.12
  476.4 7.0 copy-start.24
  476.4 7.0 copy-start.29
  476.4 7.0 copy-start.52
  483.4 4.2 copy-start.47
  751.6 6.6 copy-start.21
  (14 other events, 23.5 us)
Sparse Core Ops, SparseCore 0:
  255.7 85.3 all-reduce.4
  343.8 209.0 all-gather.2
  560.4 191.1 all-reduce.6
